TPU v7x, 32 devices: a whole 2x2x4 slice. The times are simulated.
32 devices in a mesh: grp: 2 (over y), row: 4 (over z), col: 2 (over x), slc: 2 (over core).
Axes of the slice: x: 2, y: 2, z: 4, core: 2. Of those that a mesh axis runs over, the one named last changes fastest.
Arguments:
- objects: bfloat16 [2, 2, 3072, 768], P(None, None, ('grp', 'row'), 'col'), parts along dimension 2, may hold values from -1 to 1
- probes: bfloat16 [4, 2, 256, 256], P(('grp', 'slc')), parts along dimension 0, may hold values from -3 to 3
- weights: float32 [256, 256], replicated, may hold values from 0.1 to 1
- counts: int32 [8, 2], P(('grp', 'row'), 'col'), parts along dimension 0, may hold values from 1 to 2, as said below
- offsets: int32 [8, 2, 2, 2], P(('grp', 'row'), 'col'), parts along dimension 0, may hold values from 0 to 383, as said below
- intensities: bfloat16 [8, 2, 2, 256, 256], P(('grp', 'row'), 'col'), parts along dimension 0, may hold values from 0.049804688 to 2
Outputs:
- gradient: float32 [2, 2, 3072, 768], P('slc', None, ('grp', 'row'), 'col'), parts along dimension 2
There are 2 independent parts, one for each index of `grp`. A program takes and returns all parts, laid end to end along the dimension named above; an argument that names none is the same for every part. Nothing has to cross between parts.
Inputs may be any that keep to these rules, and one draw needn't show every extreme that they name: `counts`: some tile has exactly 2 positions. `offsets`: every window of a live position lies inside the object; entries of slots at or after a tile's count are ignored.
All inputs are finite; a program needn't handle non-finite values.
Results may differ from a plain program's by a relative error of at most 0.019.
Values may be sent and summed in bfloat16 or wider, within the bound.
A program may use at most 64 MiB of HBM per device.

v0:
```python
import jax
import jax.numpy as jnp
from jax import lax
from jax.sharding import PartitionSpec as P

fresnel = 0.5


def from_behind(x, axis, by):
    count = lax.axis_size(axis)
    pairs = [(i, i + by) for i in range(count) if 0 <= i + by < count]
    return lax.ppermute(x, axis, pairs)


def dft_tables(extent):
    counter = jnp.arange(extent, dtype=jnp.int32)
    product = counter[:, None] * counter[None, :] % extent
    angles = 2.0 * jnp.pi / extent * product.astype(jnp.float32)
    norm_scale = 1.0 / jnp.sqrt(jnp.asarray(extent, jnp.float32))
    table_re = (jnp.cos(angles) * norm_scale).astype(jnp.bfloat16)
    table_im = (-jnp.sin(angles) * norm_scale).astype(jnp.bfloat16)
    return (table_re, table_im)


def chirp_factor(extent):
    counter = jnp.arange(extent, dtype=jnp.int32)
    signed_freq = (counter + extent // 2) % extent - extent // 2
    squares = (
        signed_freq[:, None] * signed_freq[:, None] + signed_freq[None, :] * signed_freq[None, :]
    )
    angles = -jnp.pi * fresnel / extent * squares.astype(jnp.float32)
    return (jnp.cos(angles), jnp.sin(angles))


def transform(real, imag, table_re, table_im):
    real_half = real.astype(jnp.bfloat16)
    imag_half = imag.astype(jnp.bfloat16)
    mid_re = jnp.dot(table_re, real_half, preferred_element_type=jnp.float32) - jnp.dot(
        table_im, imag_half, preferred_element_type=jnp.float32
    )
    mid_im = jnp.dot(table_re, imag_half, preferred_element_type=jnp.float32) + jnp.dot(
        table_im, real_half, preferred_element_type=jnp.float32
    )
    mid_re = mid_re.astype(jnp.bfloat16)
    mid_im = mid_im.astype(jnp.bfloat16)
    out_re = jnp.dot(mid_re, table_re, preferred_element_type=jnp.float32) - jnp.dot(
        mid_im, table_im, preferred_element_type=jnp.float32
    )
    out_im = jnp.dot(mid_re, table_im, preferred_element_type=jnp.float32) + jnp.dot(
        mid_im, table_re, preferred_element_type=jnp.float32
    )
    return (out_re, out_im)


def complex_mul(left_re, left_im, right_re, right_im):
    return (left_re * right_re - left_im * right_im, left_re * right_im + left_im * right_re)


def conj_mul(left_re, left_im, right_re, right_im):
    return (left_re * right_re + left_im * right_im, left_re * right_im - left_im * right_re)


def forward_mode(probe_re, probe_im, window, tables, chirps):
    table_re, table_im, inverse_im = tables
    chirp_re, chirp_im = chirps
    first_re = window[0, 0].astype(jnp.float32)
    first_im = window[0, 1].astype(jnp.float32)
    second_re = window[1, 0].astype(jnp.float32)
    second_im = window[1, 1].astype(jnp.float32)
    psi_re, psi_im = complex_mul(probe_re, probe_im, first_re, first_im)
    spec_re, spec_im = transform(psi_re, psi_im, table_re, table_im)
    spec_re, spec_im = complex_mul(chirp_re, chirp_im, spec_re, spec_im)
    prop_re, prop_im = transform(spec_re, spec_im, table_re, inverse_im)
    exit_re, exit_im = complex_mul(prop_re, prop_im, second_re, second_im)
    far_re, far_im = transform(exit_re, exit_im, table_re, table_im)
    return (prop_re, prop_im, far_re, far_im)


def backward_mode(
    probe_re, probe_im, window, prop_re, prop_im, far_re, far_im, residual, tables, chirps
):
    table_re, table_im, inverse_im = tables
    chirp_re, chirp_im = chirps
    second_re = window[1, 0].astype(jnp.float32)
    second_im = window[1, 1].astype(jnp.float32)
    back_re, back_im = transform(residual * far_re, residual * far_im, table_re, inverse_im)
    grad_two_re, grad_two_im = conj_mul(prop_re, prop_im, back_re, back_im)
    gprop_re, gprop_im = conj_mul(second_re, second_im, back_re, back_im)
    gspec_re, gspec_im = transform(gprop_re, gprop_im, table_re, table_im)
    gspec_re, gspec_im = conj_mul(chirp_re, chirp_im, gspec_re, gspec_im)
    gpsi_re, gpsi_im = transform(gspec_re, gspec_im, table_re, inverse_im)
    grad_one_re, grad_one_im = conj_mul(probe_re, probe_im, gpsi_re, gpsi_im)
    return jnp.stack([jnp.stack([grad_one_re, grad_one_im]), jnp.stack([grad_two_re, grad_two_im])])


def body(objects, probes, weights, counts, offsets, intensities):
    slices = objects.shape[0]
    tile_size = objects.shape[2]
    extent = probes.shape[2]
    table_re, table_im = dft_tables(extent)
    tables = (table_re, table_im, -table_im)
    chirps = chirp_factor(extent)
    probe_re = probes[0, 0].astype(jnp.float32)
    probe_im = probes[0, 1].astype(jnp.float32)
    from_right = from_behind(objects[:, :, :, :extent], "col", -1)
    widened = jnp.concatenate([objects, from_right], axis=3)
    from_below = from_behind(widened[:, :, :extent, :], "row", -1)
    extended = jnp.concatenate([widened, from_below], axis=2)
    tile_count = counts[0, 0]
    offset_list = offsets[0, 0]
    measured = intensities[0, 0]
    slot_limit = offset_list.shape[0]
    anchor = jnp.int32(0)

    def slot_gradient(window, data_slot):
        prop_re, prop_im, far_re, far_im = forward_mode(probe_re, probe_im, window, tables, chirps)
        intensity = lax.psum(
            (far_re * far_re + far_im * far_im).astype(jnp.bfloat16), "slc"
        ).astype(jnp.float32)
        residual = 2.0 * weights * (intensity - data_slot.astype(jnp.float32))
        return backward_mode(
            probe_re, probe_im, window, prop_re, prop_im, far_re, far_im, residual, tables, chirps
        )

    def window_at(slot_id):
        corner = offset_list[slot_id]
        return lax.dynamic_slice(
            extended, (anchor, anchor, corner[0], corner[1]), (slices, 2, extent, extent)
        )

    def add_at(gradient, slot_id, contrib):
        corner = offset_list[slot_id]
        start = (anchor, anchor, corner[0], corner[1])
        previous = lax.dynamic_slice(gradient, start, (slices, 2, extent, extent))
        return lax.dynamic_update_slice(gradient, previous + contrib, start)

    gradient = jnp.zeros(extended.shape, jnp.float32)

    def own_step(slot_id, gradient_now):
        contrib = slot_gradient(window_at(slot_id), measured[slot_id])
        contrib = jnp.where(slot_id < tile_count, contrib, jnp.zeros_like(contrib))
        return add_at(gradient_now, slot_id, contrib)

    gradient = lax.fori_loop(0, slot_limit, own_step, gradient)
    share = lax.psum_scatter(
        gradient.astype(jnp.bfloat16), "slc", scatter_dimension=0, tiled=True
    ).astype(jnp.float32)
    from_above = from_behind(share[:, :, tile_size:, :].astype(jnp.bfloat16), "row", 1).astype(
        jnp.float32
    )
    share = jnp.concatenate(
        [share[:, :, :extent, :] + from_above, share[:, :, extent:tile_size, :]], axis=2
    )
    from_left = from_behind(share[:, :, :, tile_size:].astype(jnp.bfloat16), "col", 1).astype(
        jnp.float32
    )
    return jnp.concatenate(
        [share[:, :, :, :extent] + from_left, share[:, :, :, extent:tile_size]], axis=3
    )


def solution(mesh):
    in_specs = (
        P(None, None, ("grp", "row"), "col"),
        P(("grp", "slc"), None, None, None),
        P(),
        P(("grp", "row"), "col"),
        P(("grp", "row"), "col", None, None),
        P(("grp", "row"), "col", None, None, None),
    )
    out_specs = P("slc", None, ("grp", "row"), "col")
    return jax.shard_map(body, mesh=mesh, in_specs=in_specs, out_specs=out_specs, check_vma=False)
```

profile of v0, /device:TPU:0, one launch (start us, length us, event | category | flops | bytes accessed | tf_op | source)
XLA Modules:
  0.0 331.3 jit_solution(6804542011698405931)
XLA Ops:
  7.4 1.3 slice.80
  8.7 1.3 collective-permute-start
  10.1 20.4 %collective-permute-done = bf16[2,2,384,256]{3,2,1,0:T(8,128)(2,1)S(1)} collective-permute-done((bf16[2,2,384,256]{3,2,1,0:T(8,128)(2,1)S(1)}, bf16[2,2,384,256]{3,2,1,0:T(8,128)(2,1)S(1)}, u32[]{:S(2)}, u32[]{:S(2)}) %collective-permute-start) | collective-permute-done | bytes 786464 | tf_op jit(solution)/shard_map/ppermute | solution.py:12
  30.5 1.2 slice.108
  31.7 1.3 collective-permute-start.1
  33.1 31.2 %collective-permute-done.1 = bf16[2,2,256,640]{3,2,1,0:T(8,128)(2,1)} collective-permute-done((bf16[2,2,256,640]{3,2,1,0:T(8,128)(2,1)}, bf16[2,2,256,640]{3,2,1,0:T(8,128)(2,1)}, u32[]{:S(2)}, u32[]{:S(2)}) %collective-permute-start.1) | collective-permute-done | bytes 1310752 | tf_op jit(solution)/shard_map/ppermute | solution.py:12
  64.2 3.3 %pad_maximum_fusion = bf16[2,2,640,640]{3,2,1,0:T(8,128)(2,1)} fusion(bf16[2,2,256,640]{3,2,1,0:T(8,128)(2,1)} %collective-permute-done.1, bf16[2,2,384,640]{3,2,1,0:T(8,128)(2,1)S(1)} %constant_dynamic-update-slice_fusion), kind=kLoop, calls=%fused_computation.378 | loop fusion | flops 6553600 | bytes 6553600 | tf_op jit(solution)/shard_map/concatenate | solution.py:108
  67.6 3.1 broadcast_in_dim.2
  70.7 203.0 %while.16 = (s32[]{:T(128)}, f32[2,2,640,640]{3,2,1,0:T(8,128)}, s32[2,2]{1,0:T(2,128)S(1)}, s32[]{:T(128)}, bf16[2,2,640,640]{3,2,1,0:T(8,128)(2,1)}, /*index=5...) while((s32[]{:T(128)}, f32[2,2,640,640]{3,2,1,0:T(8,128)}, ...), condition=%wide.region_2.3_spmd.clone.clone.clone, body=%wide.region_0.2_spmd.clone.clone.clone.sunk | while | flops 1673396224 | bytes 38406500 | solution.py:144
  75.6 1.2 fusion.562
  79.1 1.1 fusion.564
  84.9 2.0 fusion.569
  89.2 1.7 fusion.571
  93.2 1.1 fusion.574
  95.5 2.2 fusion.576
  103.5 1.3 fusion.581
  106.0 1.8 add_convert_fusion.2
  108.5 16.9 %all-reduce.2.cloned.1.call-done = bf16[256,256]{1,0:T(8,128)(2,1)} async-done(((bf16[256,256]{1,0:T(8,128)(2,1)}), bf16[256,256]{1,0:T(8,128)(2,1)}) %all-reduce.2.cloned.1.call-update) | async-done | bytes 131088 | tf_op jit(solution)/shard_map/while/body/eval_jaxpr/psum | solution.py:117
  132.0 1.1 fusion.587
  134.3 2.5 fusion.589
  142.6 1.1 fusion.594
  144.9 2.0 fusion.596
  149.2 1.5 fusion.598
  155.4 1.2 add_bitcast_fusion.3
  156.6 1.8 fusion.603
  158.5 12.4 %dynamic_update_slice.11 = f32[2,2,640,640]{3,2,1,0:T(8,128)} dynamic-update-slice(f32[2,2,640,640]{3,2,1,0:T(8,128)} %get-tuple-element.705, f32[2,2,256,256]{3,2,1,0:T(8,128)S(1)} %fusion.603, s32[]{:T(128)} %constant.69.clone.1..sunk, s32[]{:T(128)} %constant.69.clone.1..sunk, s32[]{:T(128)S(6)} %select_n.381, s32[]{:T(128)S(6)} %select_n.382) | dynamic-update-slice | bytes 2097156 | tf_op jit(solution)/shard_map/while/body/eval_jaxpr/dynamic_update_slice | solution.py:135
  175.7 1.2 fusion.562
  179.2 1.1 fusion.564
  184.9 2.0 fusion.569
  189.2 1.5 fusion.571
  193.1 1.1 fusion.574
  195.4 2.2 fusion.576
  203.4 1.3 fusion.581
  205.8 1.8 add_convert_fusion.2
  208.3 18.5 %all-reduce.2.cloned.1.call-done = bf16[256,256]{1,0:T(8,128)(2,1)} async-done(((bf16[256,256]{1,0:T(8,128)(2,1)}), bf16[256,256]{1,0:T(8,128)(2,1)}) %all-reduce.2.cloned.1.call-update) | async-done | bytes 131088 | tf_op jit(solution)/shard_map/while/body/eval_jaxpr/psum | solution.py:117
  235.8 2.5 fusion.589
  246.4 2.0 fusion.596
  250.7 1.5 fusion.598
  256.9 1.2 add_bitcast_fusion.3
  258.1 1.8 fusion.603
  260.0 11.9 %dynamic_update_slice.11 = f32[2,2,640,640]{3,2,1,0:T(8,128)} dynamic-update-slice(f32[2,2,640,640]{3,2,1,0:T(8,128)} %get-tuple-element.705, f32[2,2,256,256]{3,2,1,0:T(8,128)S(1)} %fusion.603, s32[]{:T(128)} %constant.69.clone.1..sunk, s32[]{:T(128)} %constant.69.clone.1..sunk, s32[]{:T(128)S(6)} %select_n.381, s32[]{:T(128)S(6)} %select_n.382) | dynamic-update-slice | bytes 2097156 | tf_op jit(solution)/shard_map/while/body/eval_jaxpr/dynamic_update_slice | solution.py:135
  273.8 4.9 %convert_element_type.492 = bf16[2,2,640,640]{3,2,1,0:T(8,128)(2,1)} convert(f32[2,2,640,640]{3,2,1,0:T(8,128)} %get-tuple-element.387) | non-fusion elementwise | flops 1638400 | bytes 9830400 | tf_op jit(solution)/shard_map/convert_element_type | solution.py:146
  278.8 13.0 %reduce-scatter.2.cloned.1.call-done = bf16[1,2,640,640]{3,2,1,0:T(8,128)(2,1)} async-done(((bf16[2,2,640,640]{3,2,1,0:T(8,128)(2,1)}), bf16[1,2,640,640]{3,2,1,0:T(8,128)(2,1)}) %reduce-scatter.2.cloned.1.call-update) | async-done | bytes 1638416 | tf_op jit(solution)/shard_map/reduce_scatter | solution.py:145
  291.8 1.3 slice.110
  293.1 3.8 %collective-permute-start.2 = (bf16[1,2,256,640]{3,2,1,0:T(8,128)(2,1)S(1)}, bf16[1,2,256,640]{3,2,1,0:T(8,128)(2,1)S(1)}, u32[]{:S(2)}, u32[]{:S(2)}) collective-permute-start(bf16[1,2,256,640]{3,2,1,0:T(8,128)(2,1)S(1)} %slice.110), channel_id=1, source_target_pairs={{0,4},{4,8},{8,12},{1,5},{5,9},{9,13},{2,6},{6,10},{10,14},{3,7},{... | collective-permute-start | bytes 1966088 | tf_op jit(solution)/shard_map/ppermute | solution.py:12
  298.2 13.0 %collective-permute-done.2 = bf16[1,2,256,640]{3,2,1,0:T(8,128)(2,1)S(1)} collective-permute-done((bf16[1,2,256,640]{3,2,1,0:T(8,128)(2,1)S(1)}, bf16[1,2,256,640]{3,2,1,0:T(8,128)(2,1)S(1)}, u32[]{:S(2)}, u32[]{:S(2)}) %collective-permute-start.2) | collective-permute-done | bytes 655392 | tf_op jit(solution)/shard_map/ppermute | solution.py:12
  311.3 3.4 %collective-permute-start.3 = (bf16[1,2,384,256]{3,2,1,0:T(8,128)(2,1)S(1)}, bf16[1,2,384,256]{3,2,1,0:T(8,128)(2,1)S(1)}, u32[]{:S(2)}, u32[]{:S(2)}) collective-permute-start(bf16[1,2,384,256]{3,2,1,0:T(8,128)(2,1)S(1)} %fusion.339), channel_id=1, source_target_pairs={{0,2},{1,3},{4,6},{5,7},{8,10},{9,11},{12,14},{13,15},{16,18},{17,... | collective-permute-start | bytes 1179656 | tf_op jit(solution)/shard_map/ppermute | solution.py:12
  314.7 7.7 %collective-permute-done.3 = bf16[1,2,384,256]{3,2,1,0:T(8,128)(2,1)S(1)} collective-permute-done((bf16[1,2,384,256]{3,2,1,0:T(8,128)(2,1)S(1)}, bf16[1,2,384,256]{3,2,1,0:T(8,128)(2,1)S(1)}, u32[]{:S(2)}, u32[]{:S(2)}) %collective-permute-start.3) | collective-permute-done | bytes 393248 | tf_op jit(solution)/shard_map/ppermute | solution.py:12
  (108 shorter events, 88.2 us)
Async XLA Ops:
  7.4 2.6 copy-start.2
  8.7 21.8 %collective-permute-start = (bf16[2,2,384,256]{3,2,1,0:T(8,128)(2,1)S(1)}, bf16[2,2,384,256]{3,2,1,0:T(8,128)(2,1)S(1)}, u32[]{:S(2)}, u32[]{:S(2)}) collective-permute-start(bf16[2,2,384,256]{3,2,1,0:T(8,128)(2,1)S(1)} %slice.80), channel_id=1, source_target_pairs={{2,0},{3,1},{6,4},{7,5},{10,8},{11,9},{14,12},{15,13},{18,16},{19,... | collective-permute-start | bytes 2359304 | tf_op jit(solution)/shard_map/ppermute | solution.py:12
  10.1 22.9 %copy-start.4 = (bf16[1,2,256,256]{3,2,1,0:T(8,128)(2,1)S(1)}, bf16[1,2,256,256]{3,2,1,0:T(8,128)(2,1)}, u32[]{:S(2)}) copy-start(bf16[1,2,256,256]{3,2,1,0:T(8,128)(2,1)} %param.9) | copy-start | bytes 786436
  31.7 32.5 %collective-permute-start.1 = (bf16[2,2,256,640]{3,2,1,0:T(8,128)(2,1)}, bf16[2,2,256,640]{3,2,1,0:T(8,128)(2,1)}, u32[]{:S(2)}, u32[]{:S(2)}) collective-permute-start(bf16[2,2,256,640]{3,2,1,0:T(8,128)(2,1)} %slice.108), channel_id=1, source_target_pairs={{4,0},{8,4},{12,8},{5,1},{9,5},{13,9},{6,2},{10,6},{14,10},{7,3},{... | collective-permute-start | bytes 3932168 | tf_op jit(solution)/shard_map/ppermute | solution.py:12
  67.6 3.1 copy-start
  67.6 3.1 copy-start.3
  67.6 3.1 copy-start.5
  71.0 54.4 %all-reduce.2.cloned.1.call-start = ((), (), s32[]{:S(2)}) async-start(), calls=%async_computation.2 | async-start | bytes 262144 | tf_op jit(solution)/shard_map/while/body/eval_jaxpr/psum | solution.py:117
  171.0 55.8 %all-reduce.2.cloned.1.call-start = ((), (), s32[]{:S(2)}) async-start(), calls=%async_computation.2 | async-start | bytes 262144 | tf_op jit(solution)/shard_map/while/body/eval_jaxpr/psum | solution.py:117
  273.8 18.0 %reduce-scatter.2.cloned.1.call-start = ((), (), s32[]{:S(2)}) async-start(), calls=%async_computation.1 | async-start | bytes 4915200 | tf_op jit(solution)/shard_map/reduce_scatter | solution.py:145
  291.8 6.1 %copy-start.1 = (bf16[1,2,640,640]{3,2,1,0:T(8,128)(2,1)S(1)}, bf16[1,2,640,640]{3,2,1,0:T(8,128)(2,1)}, u32[]{:S(2)}) copy-start(bf16[1,2,640,640]{3,2,1,0:T(8,128)(2,1)} %reduce-scatter.2.cloned.1.call-done) | copy-start | bytes 4915204
  293.1 18.1 %collective-permute-start.2 = (bf16[1,2,256,640]{3,2,1,0:T(8,128)(2,1)S(1)}, bf16[1,2,256,640]{3,2,1,0:T(8,128)(2,1)S(1)}, u32[]{:S(2)}, u32[]{:S(2)}) collective-permute-start(bf16[1,2,256,640]{3,2,1,0:T(8,128)(2,1)S(1)} %slice.110), channel_id=1, source_target_pairs={{0,4},{4,8},{8,12},{1,5},{5,9},{9,13},{2,6},{6,10},{10,14},{3,7},{... | collective-permute-start | bytes 1966088 | tf_op jit(solution)/shard_map/ppermute | solution.py:12
  311.3 11.1 %collective-permute-start.3 = (bf16[1,2,384,256]{3,2,1,0:T(8,128)(2,1)S(1)}, bf16[1,2,384,256]{3,2,1,0:T(8,128)(2,1)S(1)}, u32[]{:S(2)}, u32[]{:S(2)}) collective-permute-start(bf16[1,2,384,256]{3,2,1,0:T(8,128)(2,1)S(1)} %fusion.339), channel_id=1, source_target_pairs={{0,2},{1,3},{4,6},{5,7},{8,10},{9,11},{12,14},{13,15},{16,18},{17,... | collective-permute-start | bytes 1179656 | tf_op jit(solution)/shard_map/ppermute | solution.py:12
Sparse Core Ops, SparseCore 0:
  107.9 17.3 all-reduce.1
  207.8 19.0 all-reduce.1
Sparse Core Ops, SparseCore 1:
  278.9 12.9 reduce-scatter.1
where the time goes:
time: 335 us; the launch traced here: 331 us
  matrix products  122 us (36%)
  waiting for transfers between devices  121 us (36%)
  local copies, waits for them, and re-layouts  33.5 us (10%)
  other arithmetic  18.1 us (5%)
  between operations  15.2 us (5%)
  loops' own time  12.4 us (4%)
  starting transfers between devices  9.91 us (3%)
    ppermute x4, waiting for transfers between devices, from_behind(): return lax.ppermute(x, axis, pairs)  72.3 us
    psum x2, waiting for transfers between devices, slot_gradient(): lax.psum((far_re * far_re + far_im * far_im).astype(jnp.bfloat16), 'slc')  35.4 us
    dynamic_update_slice x2, local copies, waits for them, and re-layouts, add_at(): return lax.dynamic_update_slice(gradient, previous + contrib, start)  24.3 us
    dot_general x12, matrix products, transform(): jnp.dot(mid_im, table_im, preferred_element_type=jnp.float32)  20.2 us
    dot_general x12, matrix products, transform(): jnp.dot(mid_im, table_re, preferred_element_type=jnp.float32)  17.2 us
    dot_general x12, matrix products, transform(): jnp.dot(table_im, imag_half, preferred_element_type=jnp.float32)  15.5 us
    dot_general x12, matrix products, transform(): jnp.dot(table_im, real_half, preferred_element_type=jnp.float32)  14.1 us
    dot_general x12, matrix products, transform(): jnp.dot(mid_re, table_im, preferred_element_type=jnp.float32)  13.7 us
  transfers between devices with their start and end apart: 7, of which 7 were waited for; matrix products, arithmetic and copies ran while one was open for 0% of the time, Pallas kernels for 0%

commit v1 on v0

v1 whole, which is shorter than its diff:
```python
import functools

import jax
import jax.numpy as jnp
import ml_dtypes
import numpy as np
from jax import lax
from jax.experimental import pallas as pl
from jax.experimental.pallas import tpu as pltpu
from jax.sharding import PartitionSpec as P

MESH = pl.DeviceIdType.MESH
fresnel = 0.5
f32 = jnp.float32
bf16 = jnp.bfloat16


def dft_tables(extent):
    counter = np.arange(extent, dtype=np.int64)
    product = counter[:, None] * counter[None, :] % extent
    angles = np.float32(2.0 * np.pi / extent) * product.astype(np.float32)
    norm_scale = np.float32(1.0 / np.sqrt(extent))
    real = (np.cos(angles) * norm_scale).astype(ml_dtypes.bfloat16)
    imag = (-np.sin(angles) * norm_scale).astype(ml_dtypes.bfloat16)
    plus = np.block([[real, -imag], [imag, real]])
    minus = np.block([[real, imag], [-imag, real]])
    return np.stack([plus, minus]).astype(ml_dtypes.bfloat16)


def chirp_factor(extent):
    counter = np.arange(extent, dtype=np.int64)
    signed = (counter + extent // 2) % extent - extent // 2
    squares = signed[:, None] ** 2 + signed[None, :] ** 2
    angles = np.float32(-np.pi * fresnel / extent) * squares.astype(np.float32)
    return np.stack([np.cos(angles), np.sin(angles)]).astype(np.float32)


def cmul(a, b):
    return (a[0] * b[0] - a[1] * b[1], a[0] * b[1] + a[1] * b[0])


def conj_mul(a, b):
    return (a[0] * b[0] + a[1] * b[1], a[0] * b[1] - a[1] * b[0])


def kernel(
    shape, off_ref, cnt_ref, obj, probes, weights, intens, tables, chirps, out_ref,
    ext1, ext2, prb, wts, inten, tab, chp, gsend, gpart,
    hb, hr, hd, rb, rr, rd, lsem, fsend, frecv, relsend, relrecv, psem, gsem, hsend, hrecv,
):
    rows_n, cols_n, T, E = shape
    row, col, k = lax.axis_index("row"), lax.axis_index("col"), lax.axis_index("slc")
    other = 1 - k
    exts = (ext1, ext2)
    has_right, has_left = col < cols_n - 1, col > 0
    has_below, has_above = row < rows_n - 1, row > 0
    partner = {"slc": other}
    up, down = {"row": row - 1}, {"row": row + 1}
    left, right = {"col": col - 1}, {"col": col + 1}
    up_left = {"row": row - 1, "col": col - 1}
    down_right = {"row": row + 1, "col": col + 1}
    sides = (
        (has_right, right), (has_left, left), (has_below, down), (has_above, up),
        (has_right & has_below, down_right), (has_left & has_above, up_left),
    )

    local = [
        pltpu.make_async_copy(obj.at[0], ext1.at[:, 0:T, 0:T], lsem.at[0]),
        pltpu.make_async_copy(obj.at[1], ext2.at[:, 0:T, 0:T], lsem.at[1]),
        pltpu.make_async_copy(probes.at[0], prb.at[k], lsem.at[2]),
        pltpu.make_async_copy(weights, wts, lsem.at[3]),
        pltpu.make_async_copy(intens.at[0, 0, k], inten, lsem.at[4]),
        pltpu.make_async_copy(tables, tab, lsem.at[5]),
        pltpu.make_async_copy(chirps, chp, lsem.at[6]),
    ]
    for one in local:
        one.start()

    barrier = pltpu.get_barrier_semaphore()
    pl.semaphore_signal(barrier, inc=1, device_id=partner, device_id_type=MESH)
    for there, who in sides:
        @pl.when(there)
        def _(who=who):
            pl.semaphore_signal(barrier, inc=1, device_id=who, device_id_type=MESH)
    peers = 1
    for there, _ in sides:
        peers = peers + there.astype(jnp.int32)
    pl.semaphore_wait(barrier, peers)

    def remote(src, dst, ssem, rsem, who):
        return pltpu.make_async_remote_copy(
            src_ref=src, dst_ref=dst, send_sem=ssem, recv_sem=rsem,
            device_id=who, device_id_type=MESH,
        )

    def place(piece):
        return (
            (slice(0, T), slice(T, T + E)),
            (slice(T, T + E), slice(0, T)),
            (slice(T, T + E), slice(T, T + E)),
        )[piece]

    def source(piece):
        return (
            (slice(0, T), slice(0, E)),
            (slice(0, E), slice(0, T)),
            (slice(0, E), slice(0, E)),
        )[piece]

    sends = (has_left, has_above, has_left & has_above)
    takes = (has_right, has_below, has_right & has_below)
    targets = (left, up, up_left)

    def halo(s, piece):
        return remote(
            obj.at[(s, k) + source(piece)], exts[s].at[(k,) + place(piece)],
            fsend.at[s, piece], frecv.at[s, piece], targets[piece],
        )

    def relay(s, piece):
        region = exts[s].at[(k,) + place(piece)]
        return remote(region, region, relsend.at[s, piece], relrecv.at[s, piece], partner)

    for s in range(2):
        for piece in range(3):
            @pl.when(sends[piece])
            def _(s=s, piece=piece):
                halo(s, piece).start()

    probe_copy = remote(probes.at[0], prb.at[k], psem.at[0], psem.at[1], partner)
    probe_copy.start()

    def arrive(s):
        for piece in range(3):
            @pl.when(takes[piece])
            def _(piece=piece):
                halo(s, piece).wait_recv()
                relay(s, piece).start()
        for piece in range(3):
            @pl.when(takes[piece])
            def _(piece=piece):
                relay(s, piece).wait_recv()
            @pl.when(jnp.logical_not(takes[piece]))
            def _(piece=piece):
                at = (slice(None),) + place(piece)
                exts[s][at] = jnp.zeros_like(exts[s][at])
        local[s].wait()

    oy, ox = off_ref[0, 0, k, 0], off_ref[0, 0, k, 1]

    W = T + E

    def pick(shape_of, axis, low, wrap=False):
        here = lax.broadcasted_iota(jnp.int32, shape_of, axis)
        there = lax.broadcasted_iota(jnp.int32, shape_of, 1 - axis) + low
        if wrap:
            there = there & (E - 1)
        return jnp.where(here == there, 1.0, 0.0).astype(bf16)

    def window(s):
        by_row, by_col = pick((E, W), 1, oy), pick((W, E), 0, ox)
        result = []
        for c in range(2):
            strip = jnp.dot(by_row, exts[s][c], preferred_element_type=f32).astype(bf16)
            result.append(jnp.dot(strip, by_col, preferred_element_type=f32))
        return tuple(result)

    def transform(v, forward):
        lhs, rhs = (tab.at[0], tab.at[1]) if forward else (tab.at[1], tab.at[0])
        stacked = jnp.concatenate([v[0].astype(bf16), v[1].astype(bf16)], axis=0)
        mid = jnp.dot(lhs[...], stacked, preferred_element_type=f32).astype(bf16)
        wide = jnp.concatenate([mid[0:E], mid[E:]], axis=1)
        result = jnp.dot(wide, rhs[...], preferred_element_type=f32)
        return (result[:, 0:E], result[:, E:])

    modes = range(2)
    for one in (2, 5, 6):
        local[one].wait()
    probe_copy.wait()
    arrive(0)

    def probe(m):
        return (prb[m, 0].astype(f32), prb[m, 1].astype(f32))

    def chirp():
        return (chp[0], chp[1])

    first = window(0)
    props = []
    for m in modes:
        spec = transform(cmul(probe(m), first), True)
        props.append(transform(cmul(chirp(), spec), False))
    arrive(1)
    second = window(1)
    fars = [transform(cmul(props[m], second), True) for m in modes]
    local[3].wait()
    local[4].wait()
    intensity = sum(f[0] * f[0] + f[1] * f[1] for f in fars)
    residual = 2.0 * wts[...] * (intensity - inten[...].astype(f32))
    backs = [transform((residual * fars[m][0], residual * fars[m][1]), False) for m in modes]

    alive = jnp.zeros((E, E), jnp.int32) + k < cnt_ref[0, 0]
    turn_y, turn_x = pick((E, E), 0, oy, True), pick((E, E), 1, ox, True)

    def finish(s, parts):
        for c in range(2):
            total = jnp.where(alive, parts[0][c] + parts[1][c], 0.0).astype(bf16)
            turned = jnp.dot(turn_y, total, preferred_element_type=f32).astype(bf16)
            gsend[s, c] = jnp.dot(turned, turn_x, preferred_element_type=f32).astype(bf16)

    give = remote(gsend.at[other], gpart, gsem.at[0], gsem.at[1], partner)
    finish(1, [conj_mul(props[m], backs[m]) for m in modes])

    @pl.when(k == 0)
    def _():
        give.start()

    ones = []
    for m in modes:
        gspec = transform(conj_mul(second, backs[m]), True)
        gpsi = transform(conj_mul(chirp(), gspec), False)
        ones.append(conj_mul(probe(m), gpsi))
    finish(0, ones)

    @pl.when(k == 1)
    def _():
        give.start()

    def mask(axis, slot, start, size):
        shape_of = (size, E) if axis == 0 else (E, size)
        place_of = lax.broadcasted_iota(jnp.int32, shape_of, axis) + start
        low = off_ref[0, 0, slot, axis]
        return (place_of >= low) & (place_of < low + E)

    give.wait_recv()
    half = E // 2

    def block(c, y, x, h, w):
        y0, x0 = y % E, x % E
        total = None
        for slot, values in (
            (k, gsend[k, c, y0 : y0 + h, x0 : x0 + w].astype(f32)),
            (other, gpart[c, y0 : y0 + h, x0 : x0 + w].astype(f32)),
        ):
            ypos = lax.broadcasted_iota(jnp.int32, (h, w), 0) + y
            xpos = lax.broadcasted_iota(jnp.int32, (h, w), 1) + x
            low_y, low_x = off_ref[0, 0, slot, 0], off_ref[0, 0, slot, 1]
            inside = (
                (ypos >= low_y) & (ypos < low_y + E) & (xpos >= low_x) & (xpos < low_x + E)
            )
            term = jnp.where(inside, values, 0.0)
            total = term if total is None else total + term
        return total

    def spans(start, stop):
        result = []
        while start < stop:
            end = min(stop, (start // half + 1) * half)
            result.append((start, end - start))
            start = end
        return result

    inner, outer = spans(0, T), spans(T, T + E)

    def fill(dst, ys, xs, y_base, x_base, dtype):
        for c in range(2):
            for y, h in ys:
                for x, w in xs:
                    dst[c, y - y_base : y - y_base + h, x - x_base : x - x_base + w] = block(
                        c, y, x, h, w
                    ).astype(dtype)

    targets_out = (down_right, right, down)
    send_out = (has_right & has_below, has_right, has_below)
    take_out = (has_left & has_above, has_left, has_above)
    sources_out, lands_out = (hd, hr, hb), (rd, rr, rb)

    def push(i):
        return remote(sources_out[i], lands_out[i], hsend.at[i], hrecv.at[i], targets_out[i])

    for i, (ys, xs, yb, xb) in enumerate(
        ((outer, outer, T, T), (inner, outer, 0, T), (outer, inner, T, 0))
    ):
        @pl.when(send_out[i])
        def _(i=i, ys=ys, xs=xs, yb=yb, xb=xb):
            fill(sources_out[i], ys, xs, yb, xb, bf16)
            push(i).start()
    fill(out_ref.at[0], inner, inner, 0, 0, f32)

    areas = ((slice(0, E), slice(0, E)), (slice(0, T), slice(0, E)), (slice(0, E), slice(0, T)))
    for i in (1, 2, 0):
        @pl.when(take_out[i])
        def _(i=i):
            push(i).wait_recv()
            for c in range(2):
                at = (0, c) + areas[i]
                out_ref[at] = out_ref[at] + lands_out[i][c].astype(f32)

    for s in range(2):
        for piece in range(3):
            @pl.when(sends[piece])
            def _(s=s, piece=piece):
                halo(s, piece).wait_send()

            @pl.when(takes[piece])
            def _(s=s, piece=piece):
                relay(s, piece).wait_send()
    give.wait_send()
    for i in range(3):
        @pl.when(send_out[i])
        def _(i=i):
            push(i).wait_send()


def solution(mesh):
    rows_n, cols_n = mesh.shape["row"], mesh.shape["col"]

    def body(objects, probes, weights, counts, offsets, intensities):
        T, E = objects.shape[2], probes.shape[2]
        W = T + E
        any_space = pl.BlockSpec(memory_space=pl.ANY)
        smem = pl.BlockSpec(memory_space=pltpu.SMEM)
        dma = pltpu.SemaphoreType.DMA
        return pl.pallas_call(
            functools.partial(kernel, (rows_n, cols_n, T, E)),
            out_shape=jax.ShapeDtypeStruct((1, 2, T, T), f32),
            in_specs=[smem, smem] + [any_space] * 6,
            out_specs=pl.BlockSpec(memory_space=pltpu.VMEM),
            scratch_shapes=[
                pltpu.VMEM((2, W, W), bf16), pltpu.VMEM((2, W, W), bf16),
                pltpu.VMEM((2, 2, E, E), bf16), pltpu.VMEM((E, E), f32),
                pltpu.VMEM((E, E), bf16), pltpu.VMEM((2, 2 * E, 2 * E), bf16),
                pltpu.VMEM((2, E, E), f32),
                pltpu.VMEM((2, 2, E, E), bf16),
                pltpu.VMEM((2, E, E), bf16),
                pltpu.VMEM((2, E, T), bf16), pltpu.VMEM((2, T, E), bf16), pltpu.VMEM((2, E, E), bf16),
                pltpu.VMEM((2, E, T), bf16), pltpu.VMEM((2, T, E), bf16), pltpu.VMEM((2, E, E), bf16),
                dma((7,)), dma((2, 3)), dma((2, 3)), dma((2, 3)), dma((2, 3)),
                dma((2,)), dma((2,)), dma((3,)), dma((3,)),
            ],
            compiler_params=pltpu.CompilerParams(
                collective_id=0, has_side_effects=True, vmem_limit_bytes=48 * 1024 * 1024
            ),
            name="ptycho",
        )(
            offsets, counts, objects, probes, weights, intensities,
            jnp.asarray(dft_tables(E)), jnp.asarray(chirp_factor(E)),
        )

    in_specs = (
        P(None, None, ("grp", "row"), "col"),
        P(("grp", "slc"), None, None, None),
        P(),
        P(("grp", "row"), "col"),
        P(("grp", "row"), "col", None, None),
        P(("grp", "row"), "col", None, None, None),
    )
    out_specs = P("slc", None, ("grp", "row"), "col")
    return jax.shard_map(body, mesh=mesh, in_specs=in_specs, out_specs=out_specs, check_vma=False)
```

time: 335 us -> 53 us (0.16)
  matrix products: 122 us -> 0 us
  waiting for transfers between devices: 121 us -> 0 us
  Pallas kernels: 0 us -> 43.9 us
  local copies, waits for them, and re-layouts: 33.5 us -> 8.07 us
  other arithmetic: 18.1 us -> 0 us
  between operations: 15.2 us -> 0.67 us
  loops' own time: 12.4 us -> 0 us
  starting transfers between devices: 9.91 us -> 0 us
    dot_general x96 -> x0, matrix products: 122 us -> none  [the longest x12 20.2 us: transform(): jnp.dot(mid_im, table_im, preferred_element_type=jnp.float32)]
    ppermute x4 -> x0, waiting for transfers between devices: 72.3 us -> none  [from_behind(): return lax.ppermute(x, axis, pairs)]
    pallas_call x0 -> x1, Pallas kernels: none -> 43.9 us  [body(): pl.pallas_call(functools.partial(kernel, (rows_n, cols_n, T, E)), out_sha...]
    psum x2 -> x0, waiting for transfers between devices: 35.4 us -> none  [slot_gradient(): lax.psum((far_re * far_re + far_im * far_im).astype(jnp.bfloat16), 'slc')]
    dynamic_update_slice x2 -> x0, local copies, waits for them, and re-layouts: 24.3 us -> none  [add_at(): return lax.dynamic_update_slice(gradient, previous + contrib, start)]
    reduce_scatter x1 -> x0, waiting for transfers between devices: 13 us -> none  [body(): lax.psum_scatter(gradient.astype(jnp.bfloat16), 'slc', scatter_dimension=...]
    another operation x1 -> x0, loops' own time: 12.4 us -> none  [body(): gradient = lax.fori_loop(0, slot_limit, own_step, gradient)]
    ppermute x4 -> x0, starting transfers between devices: 9.78 us -> none  [from_behind(): return lax.ppermute(x, axis, pairs)]
  transfers between devices with their start and end apart: 7 -> 0, of which waited for: 7 -> 0; matrix products, arithmetic and copies ran while one was open for 0% -> 0% of each run, Pallas kernels for 0% -> 0%
where the time goes in v1:
time: 53 us; the launch traced here: 52.6 us
  Pallas kernels  43.9 us (83%)
  local copies, waits for them, and re-layouts  8.07 us (15%)
  between operations  0.67 us (1%)
    pallas_call x1, Pallas kernels, body(): pl.pallas_call(functools.partial(kernel, (rows_n, cols_n, T, E)), out_sha...  43.9 us
    unnamed x15, local copies, waits for them, and re-layouts  8.07 us

profile of v1, /device:TPU:0, one launch (start us, length us, event | category | flops | bytes accessed | tf_op | source)
XLA Modules:
  0.0 52.6 jit_solution(13574416684850821834)
XLA Ops:
  0.7 0.0 copy-start
  0.7 1.3 %copy-done = bf16[2,2,384,384]{3,2,1,0:T(8,128)(2,1)S(1)} copy-done((bf16[2,2,384,384]{3,2,1,0:T(8,128)(2,1)S(1)}, bf16[2,2,384,384]{3,2,1,0:T(8,128)(2,1)}, u32[]{:S(2)}) %copy-start) | copy-done | bytes 1179672
  1.9 0.0 copy-start.1
  1.9 1.2 %copy-done.1 = bf16[2,512,512]{2,1,0:T(8,128)(2,1)S(1)} copy-done((bf16[2,512,512]{2,1,0:T(8,128)(2,1)S(1)}, bf16[2,512,512]{2,1,0:T(8,128)(2,1)}, u32[]{:S(2)}) %copy-start.1) | copy-done | bytes 1048600
  3.1 0.0 copy-start.2
  3.2 1.0 %copy-done.2 = f32[2,256,256]{2,1,0:T(8,128)S(1)} copy-done((f32[2,256,256]{2,1,0:T(8,128)S(1)}, f32[2,256,256]{2,1,0:T(8,128)}, u32[]{:S(2)}) %copy-start.2) | copy-done | bytes 524312
  4.2 0.0 copy-start.3
  4.2 0.9 %copy-done.3 = bf16[1,2,256,256]{3,2,1,0:T(8,128)(2,1)S(1)} copy-done((bf16[1,2,256,256]{3,2,1,0:T(8,128)(2,1)S(1)}, bf16[1,2,256,256]{3,2,1,0:T(8,128)(2,1)}, u32[]{:S(2)}) %copy-start.3) | copy-done | bytes 262168
  5.1 0.0 copy-start.4
  5.1 0.9 %copy-done.4 = f32[256,256]{1,0:T(8,128)S(1)} copy-done((f32[256,256]{1,0:T(8,128)S(1)}, f32[256,256]{1,0:T(8,128)}, u32[]{:S(2)}) %copy-start.4) | copy-done | bytes 262168
  6.1 0.0 copy-start.5
  6.1 0.9 %copy-done.5 = bf16[1,1,2,256,256]{4,3,2,1,0:T(8,128)(2,1)S(1)} copy-done((bf16[1,1,2,256,256]{4,3,2,1,0:T(8,128)(2,1)S(1)}, bf16[1,1,2,256,256]{4,3,2,1,0:T(8,128)(2,1)}, u32[]{:S(2)}) %copy-start.5) | copy-done | bytes 262168
  7.0 0.0 copy-start.6
  7.0 0.7 %copy-done.6 = s32[1,1,2,2]{3,2,1,0:T(2,128)S(1)} copy-done((s32[1,1,2,2]{3,2,1,0:T(2,128)S(1)}, s32[1,1,2,2]{3,2,1,0:T(2,128)}, u32[]{:S(2)}) %copy-start.6) | copy-done | bytes 40
  7.7 43.9 %ptycho.1 = f32[1,2,384,384]{3,2,1,0:T(8,128)S(1)} custom-call(s32[1,1,2,2]{3,2,1,0:T(2,128)S(1)} %copy-done.6, s32[1,1]{1,0:T(1,128)S(6)} %copy.10.cnt_ref, bf16[2,2,384,384]{3,2,1,0:T(8,128)(2,1)S(1)} %copy-done, bf16[1,2,256,256]{3,2,1,0:T(8,128)(2,1)S(1)} %copy-done.3, f32[256,256]{1,0:T(8,128)S(1)} %copy-done.4, ...), custom_call_target="tpu_custom_call" | custom-call | tf_op jit(solution)/shard_map/ptycho/pallas_call | solution.py:324
  51.6 1.0 %copy.11 = f32[1,2,384,384]{3,2,1,0:T(8,128)} copy(f32[1,2,384,384]{3,2,1,0:T(8,128)S(1)} %ptycho.1) | data formatting | bytes 2359296
Async XLA Ops:
  0.7 1.3 %copy-start = (bf16[2,2,384,384]{3,2,1,0:T(8,128)(2,1)S(1)}, bf16[2,2,384,384]{3,2,1,0:T(8,128)(2,1)}, u32[]{:S(2)}) copy-start(bf16[2,2,384,384]{3,2,1,0:T(8,128)(2,1)} %obj.1) | copy-start | bytes 3538948
  1.9 1.2 %copy-start.1 = (bf16[2,512,512]{2,1,0:T(8,128)(2,1)S(1)}, bf16[2,512,512]{2,1,0:T(8,128)(2,1)}, u32[]{:S(2)}) copy-start(bf16[2,512,512]{2,1,0:T(8,128)(2,1)} %constant.4.clone.tables) | copy-start | bytes 3145732
  3.1 1.0 %copy-start.2 = (f32[2,256,256]{2,1,0:T(8,128)S(1)}, f32[2,256,256]{2,1,0:T(8,128)}, u32[]{:S(2)}) copy-start(f32[2,256,256]{2,1,0:T(8,128)} %constant.5.clone.chirps) | copy-start | bytes 1572868
  4.2 0.9 %copy-start.3 = (bf16[1,2,256,256]{3,2,1,0:T(8,128)(2,1)S(1)}, bf16[1,2,256,256]{3,2,1,0:T(8,128)(2,1)}, u32[]{:S(2)}) copy-start(bf16[1,2,256,256]{3,2,1,0:T(8,128)(2,1)} %probes.1) | copy-start | bytes 786436
  5.1 0.9 %copy-start.4 = (f32[256,256]{1,0:T(8,128)S(1)}, f32[256,256]{1,0:T(8,128)}, u32[]{:S(2)}) copy-start(f32[256,256]{1,0:T(8,128)} %weights.1) | copy-start | bytes 786436
  6.1 0.9 %copy-start.5 = (bf16[1,1,2,256,256]{4,3,2,1,0:T(8,128)(2,1)S(1)}, bf16[1,1,2,256,256]{4,3,2,1,0:T(8,128)(2,1)}, u32[]{:S(2)}) copy-start(bf16[1,1,2,256,256]{4,3,2,1,0:T(8,128)(2,1)} %intens.1) | copy-start | bytes 786436
  7.0 0.7 %copy-start.6 = (s32[1,1,2,2]{3,2,1,0:T(2,128)S(1)}, s32[1,1,2,2]{3,2,1,0:T(2,128)}, u32[]{:S(2)}) copy-start(s32[1,1,2,2]{3,2,1,0:T(2,128)} %off_ref.1) | copy-start | bytes 52

commit v2 on v1

--- a/solution.py
+++ b/solution.py
@@ -57,11 +57,8 @@
     partner = {"slc": other}
     up, down = {"row": row - 1}, {"row": row + 1}
     left, right = {"col": col - 1}, {"col": col + 1}
-    up_left = {"row": row - 1, "col": col - 1}
-    down_right = {"row": row + 1, "col": col + 1}
     sides = (
         (has_right, right), (has_left, left), (has_below, down), (has_above, up),
-        (has_right & has_below, down_right), (has_left & has_above, up_left),
     )
 
     local = [
@@ -93,62 +90,86 @@
             device_id=who, device_id_type=MESH,
         )
 
-    def place(piece):
-        return (
-            (slice(0, T), slice(T, T + E)),
-            (slice(T, T + E), slice(0, T)),
-            (slice(T, T + E), slice(T, T + E)),
-        )[piece]
-
-    def source(piece):
-        return (
-            (slice(0, T), slice(0, E)),
-            (slice(0, E), slice(0, T)),
-            (slice(0, E), slice(0, E)),
-        )[piece]
-
-    sends = (has_left, has_above, has_left & has_above)
-    takes = (has_right, has_below, has_right & has_below)
-    targets = (left, up, up_left)
+    W = T + E
+    near, rest, far = slice(0, E), slice(E, T), slice(T, W)
+    places = ((near, far), (far, near), (rest, far), (far, rest), (far, far))
+    sources = ((near, near), (near, near), (rest, near), (near, rest))
+    sends = (has_left, has_above, has_left, has_above)
+    takes = (has_right, has_below, has_right, has_below, has_right & has_below)
+    targets = (left, up, left, up)
+    turn = (has_above & has_right, has_left & has_below)
 
     def halo(s, piece):
         return remote(
-            obj.at[(s, k) + source(piece)], exts[s].at[(k,) + place(piece)],
+            obj.at[(s, k) + sources[piece]], exts[s].at[(k,) + places[piece]],
             fsend.at[s, piece], frecv.at[s, piece], targets[piece],
         )
 
+    def corner(s, core):
+        return remote(
+            exts[s].at[(core,) + places[core]], exts[s].at[(core,) + places[4]],
+            fsend.at[s, 4], frecv.at[s, 4], targets[1 - core],
+        )
+
     def relay(s, piece):
-        region = exts[s].at[(k,) + place(piece)]
+        region = exts[s].at[(k,) + places[piece]]
         return remote(region, region, relsend.at[s, piece], relrecv.at[s, piece], partner)
 
-    for s in range(2):
-        for piece in range(3):
+    def start(s):
+        for piece in range(4):
             @pl.when(sends[piece])
-            def _(s=s, piece=piece):
+            def _(piece=piece):
                 halo(s, piece).start()
 
-    probe_copy = remote(probes.at[0], prb.at[k], psem.at[0], psem.at[1], partner)
-    probe_copy.start()
+    def hand_over(s, piece):
+        @pl.when(takes[piece])
+        def _():
+            if piece < 4:
+                halo(s, piece).wait_recv()
+            else:
+                corner(s, 0).wait_recv()
+            relay(s, piece).start()
+
+    def early(s):
+        for core in range(2):
+            @pl.when(k == core)
+            def _(core=core):
+                hand_over(s, core)
+
+                @pl.when(turn[core])
+                def _():
+                    corner(s, core).start()
 
     def arrive(s):
-        for piece in range(3):
-            @pl.when(takes[piece])
-            def _(piece=piece):
-                halo(s, piece).wait_recv()
-                relay(s, piece).start()
-        for piece in range(3):
+        for core in range(2):
+            @pl.when(k == core)
+            def _(core=core):
+                hand_over(s, 1 - core)
+        for piece in (2, 3, 4):
+            hand_over(s, piece)
+        for piece in range(5):
             @pl.when(takes[piece])
             def _(piece=piece):
                 relay(s, piece).wait_recv()
-            @pl.when(jnp.logical_not(takes[piece]))
-            def _(piece=piece):
-                at = (slice(None),) + place(piece)
-                exts[s][at] = jnp.zeros_like(exts[s][at])
         local[s].wait()
 
+    start(0)
+    probe_copy = remote(probes.at[0], prb.at[k], psem.at[0], psem.at[1], partner)
+    probe_copy.start()
+    for one in (2, 5, 6):
+        local[one].wait()
+    for there, at in (
+        (has_right, (slice(0, T), far)),
+        (has_below, (far, slice(0, T))),
+        (has_right & has_below, (far, far)),
+    ):
+        @pl.when(jnp.logical_not(there))
+        def _(at=at):
+            for ext in exts:
+                for c in range(2):
+                    ext[(c,) + at] = jnp.zeros_like(ext[(c,) + at])
+
     oy, ox = off_ref[0, 0, k, 0], off_ref[0, 0, k, 1]
-
-    W = T + E
 
     def pick(shape_of, axis, low, wrap=False):
         here = lax.broadcasted_iota(jnp.int32, shape_of, axis)
@@ -174,8 +195,8 @@
         return (result[:, 0:E], result[:, E:])
 
     modes = range(2)
-    for one in (2, 5, 6):
-        local[one].wait()
+    early(0)
+    start(1)
     probe_copy.wait()
     arrive(0)
 
@@ -190,6 +211,8 @@
     for m in modes:
         spec = transform(cmul(probe(m), first), True)
         props.append(transform(cmul(chirp(), spec), False))
+        if m == 0:
+            early(1)
     arrive(1)
     second = window(1)
     fars = [transform(cmul(props[m], second), True) for m in modes]
@@ -215,24 +238,6 @@
     def _():
         give.start()
 
-    ones = []
-    for m in modes:
-        gspec = transform(conj_mul(second, backs[m]), True)
-        gpsi = transform(conj_mul(chirp(), gspec), False)
-        ones.append(conj_mul(probe(m), gpsi))
-    finish(0, ones)
-
-    @pl.when(k == 1)
-    def _():
-        give.start()
-
-    def mask(axis, slot, start, size):
-        shape_of = (size, E) if axis == 0 else (E, size)
-        place_of = lax.broadcasted_iota(jnp.int32, shape_of, axis) + start
-        low = off_ref[0, 0, slot, axis]
-        return (place_of >= low) & (place_of < low + E)
-
-    give.wait_recv()
     half = E // 2
 
     def block(c, y, x, h, w):
@@ -262,51 +267,119 @@
 
     inner, outer = spans(0, T), spans(T, T + E)
 
-    def fill(dst, ys, xs, y_base, x_base, dtype):
-        for c in range(2):
-            for y, h in ys:
-                for x, w in xs:
-                    dst[c, y - y_base : y - y_base + h, x - x_base : x - x_base + w] = block(
-                        c, y, x, h, w
-                    ).astype(dtype)
-
-    targets_out = (down_right, right, down)
-    send_out = (has_right & has_below, has_right, has_below)
-    take_out = (has_left & has_above, has_left, has_above)
-    sources_out, lands_out = (hd, hr, hb), (rd, rr, rb)
+    def fill(dst, c, ys, xs, y_base, x_base, dtype):
+        for y, h in ys:
+            for x, w in xs:
+                dst[y - y_base : y - y_base + h, x - x_base : x - x_base + w] = block(
+                    c, y, x, h, w
+                ).astype(dtype)
 
     def push(i):
-        return remote(sources_out[i], lands_out[i], hsend.at[i], hrecv.at[i], targets_out[i])
-
-    for i, (ys, xs, yb, xb) in enumerate(
-        ((outer, outer, T, T), (inner, outer, 0, T), (outer, inner, T, 0))
+        src, dst, who = (
+            (hd.at[0], rd.at[0], down), (hd.at[1], rd.at[1], right),
+            (hb.at[0], rb.at[0], down), (hr.at[1], rr.at[1], right),
+            (hb.at[1], rb.at[1], down), (hr.at[0], rr.at[0], right),
+        )[i]
+        return remote(src, dst, hsend.at[i], hrecv.at[i], who)
+
+    both_out = has_right & has_below
+    send_out = (both_out, both_out, has_below, has_right, has_below, has_right)
+
+    def deliver_first():
+        give.wait_recv()
+
+        @pl.when(both_out)
+        def _():
+            for c in range(2):
+                fill(hd.at[c], c, outer, outer, T, T, bf16)
+                push(c).start()
+
+        @pl.when(has_below)
+        def _():
+            fill(hb.at[0], 0, outer, inner, T, 0, bf16)
+            push(2).start()
+
+        @pl.when(has_right)
+        def _():
+            fill(hr.at[1], 1, inner, outer, 0, T, bf16)
+            push(3).start()
+
+        @pl.when(has_below)
+        def _():
+            fill(hb.at[1], 1, outer, inner, T, 0, bf16)
+
+        @pl.when(has_right)
+        def _():
+            fill(hr.at[0], 0, inner, outer, 0, T, bf16)
+
+    def deliver_second():
+        @pl.when(has_below)
+        def _():
+            @pl.when(has_left)
+            def _():
+                push(1).wait_recv()
+                hb[1, :, 0:E] = (hb[1, :, 0:E].astype(f32) + rd[1].astype(f32)).astype(bf16)
+
+            push(4).start()
+
+        @pl.when(has_right)
+        def _():
+            @pl.when(has_above)
+            def _():
+                push(0).wait_recv()
+                hr[0, 0:E, :] = (hr[0, 0:E, :].astype(f32) + rd[0].astype(f32)).astype(bf16)
+
+            push(5).start()
+
+    gspecs = [transform(conj_mul(second, backs[m]), True) for m in modes]
+
+    @pl.when(k == 1)
+    def _():
+        deliver_first()
+
+    finish(0, [
+        conj_mul(probe(m), transform(conj_mul(chirp(), gspecs[m]), False)) for m in modes
+    ])
+
+    @pl.when(k == 1)
+    def _():
+        give.start()
+
+    @pl.when(k == 0)
+    def _():
+        deliver_first()
+
+    deliver_second()
+    for c in range(2):
+        fill(out_ref.at[0, c], c, inner, inner, 0, 0, f32)
+
+    for i, c, there, land, area in (
+        (2, 0, has_above, rb, (near, slice(0, T))),
+        (3, 1, has_left, rr, (slice(0, T), near)),
+        (4, 1, has_above, rb, (near, slice(0, T))),
+        (5, 0, has_left, rr, (slice(0, T), near)),
     ):
-        @pl.when(send_out[i])
-        def _(i=i, ys=ys, xs=xs, yb=yb, xb=xb):
-            fill(sources_out[i], ys, xs, yb, xb, bf16)
-            push(i).start()
-    fill(out_ref.at[0], inner, inner, 0, 0, f32)
-
-    areas = ((slice(0, E), slice(0, E)), (slice(0, T), slice(0, E)), (slice(0, E), slice(0, T)))
-    for i in (1, 2, 0):
-        @pl.when(take_out[i])
-        def _(i=i):
+        @pl.when(there)
+        def _(i=i, c=c, land=land, area=area):
             push(i).wait_recv()
-            for c in range(2):
-                at = (0, c) + areas[i]
-                out_ref[at] = out_ref[at] + lands_out[i][c].astype(f32)
+            at = (0, c) + area
+            out_ref[at] = out_ref[at] + land[c].astype(f32)
 
     for s in range(2):
-        for piece in range(3):
+        for piece in range(4):
             @pl.when(sends[piece])
             def _(s=s, piece=piece):
                 halo(s, piece).wait_send()
-
+        for piece in range(5):
             @pl.when(takes[piece])
             def _(s=s, piece=piece):
                 relay(s, piece).wait_send()
+        for core in range(2):
+            @pl.when((k == core) & turn[core])
+            def _(s=s, core=core):
+                corner(s, core).wait_send()
     give.wait_send()
-    for i in range(3):
+    for i in range(6):
         @pl.when(send_out[i])
         def _(i=i):
             push(i).wait_send()
@@ -335,11 +408,11 @@
                 pltpu.VMEM((2, E, E), bf16),
                 pltpu.VMEM((2, E, T), bf16), pltpu.VMEM((2, T, E), bf16), pltpu.VMEM((2, E, E), bf16),
                 pltpu.VMEM((2, E, T), bf16), pltpu.VMEM((2, T, E), bf16), pltpu.VMEM((2, E, E), bf16),
-                dma((7,)), dma((2, 3)), dma((2, 3)), dma((2, 3)), dma((2, 3)),
-                dma((2,)), dma((2,)), dma((3,)), dma((3,)),
+                dma((7,)), dma((2, 5)), dma((2, 5)), dma((2, 5)), dma((2, 5)),
+                dma((2,)), dma((2,)), dma((6,)), dma((6,)),
             ],
             compiler_params=pltpu.CompilerParams(
-                collective_id=0, has_side_effects=True, vmem_limit_bytes=48 * 1024 * 1024
+                collective_id=0, has_side_effects=True, vmem_limit_bytes=63 * 1024 * 1024
             ),
             name="ptycho",
         )(

time: 53 us -> 43.4 us (0.82)
  local copies, waits for them, and re-layouts: 8.07 us -> 2.36 us
  Pallas kernels: 43.9 us -> 40.2 us
    unnamed x15 -> x1, local copies, waits for them, and re-layouts: 8.07 us -> 2.36 us
    pallas_call x1, Pallas kernels: 43.9 us -> 40.2 us  [body(): pl.pallas_call(functools.partial(kernel, (rows_n, cols_n, T, E)), out_sha...]
where the time goes in v2:
time: 43.4 us; the launch traced here: 43.3 us
  Pallas kernels  40.2 us (93%)
  local copies, waits for them, and re-layouts  2.36 us (5%)
  between operations  0.66 us (2%)
    pallas_call x1, Pallas kernels, body(): pl.pallas_call(functools.partial(kernel, (rows_n, cols_n, T, E)), out_sha...  40.2 us
    unnamed x1, local copies, waits for them, and re-layouts  2.36 us

profile of v2, /device:TPU:0, one launch (start us, length us, event | category | flops | bytes accessed | tf_op | source)
XLA Modules:
  0.0 43.3 jit_solution(5983183486314404141)
XLA Ops:
  0.7 40.2 %ptycho.1 = f32[1,2,384,384]{3,2,1,0:T(8,128)} custom-call(s32[1,1,2,2]{3,2,1,0:T(2,128)} %off_ref.1, s32[1,1]{1,0:T(1,128)S(6)} %copy.10.cnt_ref, bf16[2,2,384,384]{3,2,1,0:T(8,128)(2,1)} %obj.1, bf16[1,2,256,256]{3,2,1,0:T(8,128)(2,1)} %probes.1, f32[256,256]{1,0:T(8,128)} %weights.1, bf16[1,1,2,256,256]{4,3,2,1,0:T(8,128)(2,1)} %intens.1, ...), custom_call_target="tpu_custom_call" | custom-call | tf_op jit(solution)/shard_map/ptycho/pallas_call | solution.py:397
  40.9 2.4 %copy.11 = f32[1,2,384,384]{3,2,1,0:T(8,128)} copy(f32[1,2,384,384]{3,2,1,0:T(8,128)} %ptycho.1) | data formatting | bytes 2359296

commit v3 on v2

--- a/solution.py
+++ b/solution.py
@@ -140,18 +140,17 @@
                 def _():
                     corner(s, core).start()
 
-    def arrive(s):
+    def other_corner(s):
         for core in range(2):
             @pl.when(k == core)
             def _(core=core):
                 hand_over(s, 1 - core)
-        for piece in (2, 3, 4):
-            hand_over(s, piece)
-        for piece in range(5):
+
+    def landed(s, pieces):
+        for piece in pieces:
             @pl.when(takes[piece])
             def _(piece=piece):
                 relay(s, piece).wait_recv()
-        local[s].wait()
 
     start(0)
     probe_copy = remote(probes.at[0], prb.at[k], psem.at[0], psem.at[1], partner)
@@ -178,13 +177,31 @@
             there = there & (E - 1)
         return jnp.where(here == there, 1.0, 0.0).astype(bf16)
 
-    def window(s):
-        by_row, by_col = pick((E, W), 1, oy), pick((W, E), 0, ox)
+    low = slice(0, T)
+    row_low, row_far = pick((E, T), 1, oy), pick((E, E), 1, oy - T)
+    col_low, col_far = pick((T, E), 0, ox), pick((E, E), 0, ox - T)
+
+    def part(s, by_row, by_col, at):
         result = []
         for c in range(2):
-            strip = jnp.dot(by_row, exts[s][c], preferred_element_type=f32).astype(bf16)
-            result.append(jnp.dot(strip, by_col, preferred_element_type=f32))
+            strip = jnp.dot(by_row, exts[s][(c,) + at], preferred_element_type=f32)
+            result.append(jnp.dot(strip.astype(bf16), by_col, preferred_element_type=f32))
         return tuple(result)
+
+    def plus(x, y):
+        return (x[0] + y[0], x[1] + y[1])
+
+    def window(s):
+        for piece in (2, 3):
+            hand_over(s, piece)
+        landed(s, (0, 1, 2, 3))
+        sides = plus(
+            part(s, row_low, col_far, (low, far)), part(s, row_far, col_low, (far, low))
+        )
+        sides = plus(owns[s], sides)
+        hand_over(s, 4)
+        landed(s, (4,))
+        return plus(sides, part(s, row_far, col_far, (far, far)))
 
     def transform(v, forward):
         lhs, rhs = (tab.at[0], tab.at[1]) if forward else (tab.at[1], tab.at[0])
@@ -195,10 +212,14 @@
         return (result[:, 0:E], result[:, E:])
 
     modes = range(2)
+    owns = []
+    for s in range(2):
+        local[s].wait()
+        owns.append(part(s, row_low, col_low, (low, low)))
     early(0)
     start(1)
+    other_corner(0)
     probe_copy.wait()
-    arrive(0)
 
     def probe(m):
         return (prb[m, 0].astype(f32), prb[m, 1].astype(f32))
@@ -213,7 +234,7 @@
         props.append(transform(cmul(chirp(), spec), False))
         if m == 0:
             early(1)
-    arrive(1)
+            other_corner(1)
     second = window(1)
     fars = [transform(cmul(props[m], second), True) for m in modes]
     local[3].wait()

time: 43.4 us -> 42.1 us (0.970)
  Pallas kernels: 40.2 us -> 38.9 us
    pallas_call x1, Pallas kernels: 40.2 us -> 38.9 us  [body(): pl.pallas_call(functools.partial(kernel, (rows_n, cols_n, T, E)), out_sha...]
where the time goes in v3:
time: 42.1 us; the launch traced here: 42 us
  Pallas kernels  38.9 us (92%)
  local copies, waits for them, and re-layouts  2.36 us (6%)
  between operations  0.66 us (2%)
    pallas_call x1, Pallas kernels, body(): pl.pallas_call(functools.partial(kernel, (rows_n, cols_n, T, E)), out_sha...  38.9 us
    unnamed x1, local copies, waits for them, and re-layouts  2.36 us

profile of v3, /device:TPU:0, one launch (start us, length us, event | category | flops | bytes accessed | tf_op | source)
XLA Modules:
  0.0 42.0 jit_solution(10881452526880445615)
XLA Ops:
  0.7 38.9 %ptycho.1 = f32[1,2,384,384]{3,2,1,0:T(8,128)} custom-call(s32[1,1,2,2]{3,2,1,0:T(2,128)} %off_ref.1, s32[1,1]{1,0:T(1,128)S(6)} %copy.10.cnt_ref, bf16[2,2,384,384]{3,2,1,0:T(8,128)(2,1)} %obj.1, bf16[1,2,256,256]{3,2,1,0:T(8,128)(2,1)} %probes.1, f32[256,256]{1,0:T(8,128)} %weights.1, bf16[1,1,2,256,256]{4,3,2,1,0:T(8,128)(2,1)} %intens.1, ...), custom_call_target="tpu_custom_call" | custom-call | tf_op jit(solution)/shard_map/ptycho/pallas_call | solution.py:418
  39.6 2.4 %copy.11 = f32[1,2,384,384]{3,2,1,0:T(8,128)} copy(f32[1,2,384,384]{3,2,1,0:T(8,128)} %ptycho.1) | data formatting | bytes 2359296

commit v4 on v3

--- a/solution.py
+++ b/solution.py
@@ -246,18 +246,20 @@
     alive = jnp.zeros((E, E), jnp.int32) + k < cnt_ref[0, 0]
     turn_y, turn_x = pick((E, E), 0, oy, True), pick((E, E), 1, ox, True)
 
+    def give(c):
+        return remote(gsend.at[other, c], gpart.at[c], gsem.at[c], gsem.at[2 + c], partner)
+
     def finish(s, parts):
         for c in range(2):
             total = jnp.where(alive, parts[0][c] + parts[1][c], 0.0).astype(bf16)
             turned = jnp.dot(turn_y, total, preferred_element_type=f32).astype(bf16)
             gsend[s, c] = jnp.dot(turned, turn_x, preferred_element_type=f32).astype(bf16)
 
-    give = remote(gsend.at[other], gpart, gsem.at[0], gsem.at[1], partner)
+            @pl.when(k == 1 - s)
+            def _():
+                give(c).start()
+
     finish(1, [conj_mul(props[m], backs[m]) for m in modes])
-
-    @pl.when(k == 0)
-    def _():
-        give.start()
 
     half = E // 2
 
@@ -307,11 +309,11 @@
     send_out = (both_out, both_out, has_below, has_right, has_below, has_right)
 
     def deliver_first():
-        give.wait_recv()
-
-        @pl.when(both_out)
-        def _():
-            for c in range(2):
+        for c in range(2):
+            give(c).wait_recv()
+
+            @pl.when(both_out)
+            def _():
                 fill(hd.at[c], c, outer, outer, T, T, bf16)
                 push(c).start()
 
@@ -325,17 +327,11 @@
             fill(hr.at[1], 1, inner, outer, 0, T, bf16)
             push(3).start()
 
+    def deliver_second():
         @pl.when(has_below)
         def _():
             fill(hb.at[1], 1, outer, inner, T, 0, bf16)
 
-        @pl.when(has_right)
-        def _():
-            fill(hr.at[0], 0, inner, outer, 0, T, bf16)
-
-    def deliver_second():
-        @pl.when(has_below)
-        def _():
             @pl.when(has_left)
             def _():
                 push(1).wait_recv()
@@ -345,6 +341,8 @@
 
         @pl.when(has_right)
         def _():
+            fill(hr.at[0], 0, inner, outer, 0, T, bf16)
+
             @pl.when(has_above)
             def _():
                 push(0).wait_recv()
@@ -361,10 +359,6 @@
     finish(0, [
         conj_mul(probe(m), transform(conj_mul(chirp(), gspecs[m]), False)) for m in modes
     ])
-
-    @pl.when(k == 1)
-    def _():
-        give.start()
 
     @pl.when(k == 0)
     def _():
@@ -399,7 +393,8 @@
             @pl.when((k == core) & turn[core])
             def _(s=s, core=core):
                 corner(s, core).wait_send()
-    give.wait_send()
+    for c in range(2):
+        give(c).wait_send()
     for i in range(6):
         @pl.when(send_out[i])
         def _(i=i):
@@ -430,7 +425,7 @@
                 pltpu.VMEM((2, E, T), bf16), pltpu.VMEM((2, T, E), bf16), pltpu.VMEM((2, E, E), bf16),
                 pltpu.VMEM((2, E, T), bf16), pltpu.VMEM((2, T, E), bf16), pltpu.VMEM((2, E, E), bf16),
                 dma((7,)), dma((2, 5)), dma((2, 5)), dma((2, 5)), dma((2, 5)),
-                dma((2,)), dma((2,)), dma((6,)), dma((6,)),
+                dma((2,)), dma((4,)), dma((6,)), dma((6,)),
             ],
             compiler_params=pltpu.CompilerParams(
                 collective_id=0, has_side_effects=True, vmem_limit_bytes=63 * 1024 * 1024

time: 42.1 us -> 42.2 us (level)
  no operation moved by 1% of the time
where the time goes in v4:
time: 42.2 us; the launch traced here: 42 us
  Pallas kernels  39 us (92%)
  local copies, waits for them, and re-layouts  2.36 us (6%)
  between operations  0.66 us (2%)
    pallas_call x1, Pallas kernels, body(): pl.pallas_call(functools.partial(kernel, (rows_n, cols_n, T, E)), out_sha...  39 us
    unnamed x1, local copies, waits for them, and re-layouts  2.36 us

profile of v4, /device:TPU:0, one launch (start us, length us, event | category | flops | bytes accessed | tf_op | source)
XLA Modules:
  0.0 42.0 jit_solution(3632017121334581152)
XLA Ops:
  0.7 39.0 %ptycho.1 = f32[1,2,384,384]{3,2,1,0:T(8,128)} custom-call(s32[1,1,2,2]{3,2,1,0:T(2,128)} %off_ref.1, s32[1,1]{1,0:T(1,128)S(6)} %copy.10.cnt_ref, bf16[2,2,384,384]{3,2,1,0:T(8,128)(2,1)} %obj.1, bf16[1,2,256,256]{3,2,1,0:T(8,128)(2,1)} %probes.1, f32[256,256]{1,0:T(8,128)} %weights.1, bf16[1,1,2,256,256]{4,3,2,1,0:T(8,128)(2,1)} %intens.1, ...), custom_call_target="tpu_custom_call" | custom-call | tf_op jit(solution)/shard_map/ptycho/pallas_call | solution.py:413
  39.6 2.4 %copy.11 = f32[1,2,384,384]{3,2,1,0:T(8,128)} copy(f32[1,2,384,384]{3,2,1,0:T(8,128)} %ptycho.1) | data formatting | bytes 2359296

commit v5 on v4

--- a/solution.py
+++ b/solution.py
@@ -115,9 +115,9 @@
         region = exts[s].at[(k,) + places[piece]]
         return remote(region, region, relsend.at[s, piece], relrecv.at[s, piece], partner)
 
-    def start(s):
+    def start(s, link=None):
         for piece in range(4):
-            @pl.when(sends[piece])
+            @pl.when(sends[piece] if link is None else sends[piece] & (link == piece % 2))
             def _(piece=piece):
                 halo(s, piece).start()
 
@@ -153,6 +153,7 @@
                 relay(s, piece).wait_recv()
 
     start(0)
+    start(1, k)
     probe_copy = remote(probes.at[0], prb.at[k], psem.at[0], psem.at[1], partner)
     probe_copy.start()
     for one in (2, 5, 6):
@@ -217,7 +218,7 @@
         local[s].wait()
         owns.append(part(s, row_low, col_low, (low, low)))
     early(0)
-    start(1)
+    start(1, 1 - k)
     other_corner(0)
     probe_copy.wait()
 

time: 42.2 us -> 42.6 us (level)
    pallas_call x1, Pallas kernels: 39 us -> 39.4 us  [body(): pl.pallas_call(functools.partial(kernel, (rows_n, cols_n, T, E)), out_sha...]
where the time goes in v5:
time: 42.6 us; the launch traced here: 42.4 us
  Pallas kernels  39.4 us (92%)
  local copies, waits for them, and re-layouts  2.36 us (6%)
  between operations  0.66 us (2%)
    pallas_call x1, Pallas kernels, body(): pl.pallas_call(functools.partial(kernel, (rows_n, cols_n, T, E)), out_sha...  39.4 us
    unnamed x1, local copies, waits for them, and re-layouts  2.36 us

profile of v5, /device:TPU:0, one launch (start us, length us, event | category | flops | bytes accessed | tf_op | source)
XLA Modules:
  0.0 42.4 jit_solution(10204199688408951771)
XLA Ops:
  0.7 39.4 %ptycho.1 = f32[1,2,384,384]{3,2,1,0:T(8,128)} custom-call(s32[1,1,2,2]{3,2,1,0:T(2,128)} %off_ref.1, s32[1,1]{1,0:T(1,128)S(6)} %copy.10.cnt_ref, bf16[2,2,384,384]{3,2,1,0:T(8,128)(2,1)} %obj.1, bf16[1,2,256,256]{3,2,1,0:T(8,128)(2,1)} %probes.1, f32[256,256]{1,0:T(8,128)} %weights.1, bf16[1,1,2,256,256]{4,3,2,1,0:T(8,128)(2,1)} %intens.1, ...), custom_call_target="tpu_custom_call" | custom-call | tf_op jit(solution)/shard_map/ptycho/pallas_call | solution.py:414
  40.1 2.4 %copy.11 = f32[1,2,384,384]{3,2,1,0:T(8,128)} copy(f32[1,2,384,384]{3,2,1,0:T(8,128)} %ptycho.1) | data formatting | bytes 2359296
